TPU v7x, 32 devices: a whole 2x2x4 slice. The times are simulated.
32 devices in a mesh: groups: 2 (over y), frames: 4 (over z), fsdp: 2 (over x), heads: 2 (over core).
Axes of the slice: x: 2, y: 2, z: 4, core: 2. Of those that a mesh axis runs over, the one named last changes fastest.
Arguments:
- frames_in: bfloat16 [4, 768, 1536], P(('groups', 'fsdp'), 'frames', 'heads'), parts along dimension 0, may hold values from -6 to 6
- lengths: int32 [4], P(('groups', 'fsdp')), parts along dimension 0, may hold values from 192 to 768, as said below
- w_query: bfloat16 [1536, 768], P(('frames', 'fsdp'), 'heads')
- w_key: bfloat16 [1536, 768], P(('frames', 'fsdp'), 'heads'), may hold values from -0.15625 to 0.15625
- w_value: bfloat16 [1536, 768], P(('frames', 'fsdp'), 'heads'), may hold values from -0.15625 to 0.15625
- w_out: bfloat16 [768, 1536], P('heads', ('frames', 'fsdp')), may hold values from -0.21875 to 0.21875
- w_glu: bfloat16 [1536, 2, 1536], P('fsdp', None, 'heads'), may hold values from -0.15625 to 0.15625
- dw_kernel: bfloat16 [31, 1536], P(None, 'heads'), may hold values from -1 to 1
- w_pw: bfloat16 [1536, 1536], P('heads', 'fsdp'), may hold values from -0.15625 to 0.15625
Outputs:
- block_out: bfloat16 [4, 768, 1536], P(('groups', 'fsdp'), 'frames', 'heads'), parts along dimension 0
There are 2 independent parts, one for each index of `groups`. A program takes and returns all parts, laid end to end along the dimension named above; an argument that names none is the same for every part. Nothing has to cross between parts.
Inputs may be any that keep to these rules, and one draw needn't show every extreme that they name: `lengths`: each utterance counts at least 192 valid frames, and in every group some utterance is valid over all 768 frames.
All inputs are finite; a program needn't handle non-finite values.
Results may differ from a plain program's by a relative error of at most 0.012.
The roundings to bfloat16 on the way count: a program that leaves them out, or rounds other values in their place, can miss the bound.
Values may be sent and summed in bfloat16 or wider, within the bound.
No kernel may reach another device: no remote copies, remote signals or barrier semaphores. Data moves between devices by JAX's collectives and lax.ppermute only.
A program may use at most 64 MiB of HBM per device.

v0:
```python
import math
import jax
import jax.numpy as jnp
from jax import lax
from jax.sharding import PartitionSpec as P

HEAD_DIM = 96
KERNEL = 31
EPS = 1e-05
NEG_FILL = -1e30


def padded_2(cells, sides, width):
    for axis, dim in sides:
        count = lax.axis_size(axis)
        ends = count - 1
        head = lax.slice_in_dim(cells, 0, width, axis=dim)
        tail = lax.slice_in_dim(cells, cells.shape[dim] - width, cells.shape[dim], axis=dim)
        cells = jnp.concatenate(
            [
                lax.ppermute(tail, axis, [(i, (i + 1) % count) for i in range(ends)]),
                cells,
                lax.ppermute(head, axis, [((i + 1) % count, i) for i in range(ends)]),
            ],
            axis=dim,
        )
    return cells


def layer_norm(rows):
    values = rows.astype(jnp.float32)
    mean_row = jnp.mean(values, axis=-1, keepdims=True)
    centred = values - mean_row
    variance = jnp.mean(centred * centred, axis=-1, keepdims=True)
    return centred * lax.rsqrt(variance + EPS)


def shards(frames_in, lengths, w_query, w_key, w_value, w_out, w_glu, dw_kernel, w_pw):
    full_rows = lax.all_gather(frames_in, "heads", axis=2, tiled=True)[0]
    frame_count = full_rows.shape[0]
    half_width = frames_in.shape[2]
    own_start = lax.axis_index("heads") * half_width
    normed = layer_norm(full_rows).astype(jnp.bfloat16)
    att_cols = w_query.shape[1]
    pieces = (
        lax.all_gather(w_query, ("frames", "fsdp"), axis=0, tiled=True),
        lax.all_gather(w_key, ("frames", "fsdp"), axis=0, tiled=True),
        lax.all_gather(w_value, ("frames", "fsdp"), axis=0, tiled=True),
    )
    sliced = normed
    projected = tuple(
        (jnp.dot(sliced, piece_part, preferred_element_type=jnp.float32) for piece_part in pieces)
    )
    head_count = att_cols // HEAD_DIM
    queries = projected[0].astype(jnp.bfloat16).reshape(frame_count, head_count, HEAD_DIM)
    key_rows = projected[1].astype(jnp.bfloat16)
    value_rows = projected[2].astype(jnp.bfloat16)
    length = lengths[0]
    scale_factor = 1.0 / math.sqrt(HEAD_DIM)
    start_max = jnp.full((frame_count, head_count), NEG_FILL, jnp.float32)
    pieces = (
        lax.all_gather(key_rows, "frames", axis=0, tiled=True),
        lax.all_gather(value_rows, "frames", axis=0, tiled=True),
    )
    key_block = pieces[0].reshape(-1, head_count, HEAD_DIM)
    value_block = pieces[1].reshape(-1, head_count, HEAD_DIM)
    block_rows = key_block.shape[0]
    scores = (
        jnp.einsum("qhd,khd->qhk", queries, key_block, preferred_element_type=jnp.float32)
        * scale_factor
    )
    valid = jnp.arange(block_rows, dtype=jnp.int32) < length
    masked = jnp.where(valid, scores, NEG_FILL)
    new_max = jnp.maximum(start_max, jnp.max(masked, axis=2))
    expo = jnp.where(valid, jnp.exp(masked - new_max[:, :, None]), 0.0)
    new_sum = jnp.sum(expo, axis=2)
    block_acc = jnp.einsum(
        "qhk,khd->qhd", expo.astype(jnp.bfloat16), value_block, preferred_element_type=jnp.float32
    )
    context = (block_acc / new_sum[:, :, None]).reshape(frame_count, att_cols).astype(jnp.bfloat16)
    partial_value = jnp.dot(
        context,
        lax.all_gather(w_out, ("frames", "fsdp"), axis=1, tiled=True),
        preferred_element_type=jnp.float32,
    )
    total = lax.psum(partial_value.astype(jnp.bfloat16), "heads").astype(jnp.float32)
    stream_full = (full_rows.astype(jnp.float32) + total).astype(jnp.bfloat16)
    stream_own = lax.dynamic_slice_in_dim(stream_full, own_start, half_width, 1)
    normed_two = layer_norm(stream_full).astype(jnp.bfloat16)
    channels = w_glu.shape[2]
    sliced = normed_two
    glu_pre = jnp.einsum(
        "td,dgc->tgc",
        sliced,
        lax.all_gather(w_glu, "fsdp", axis=0, tiled=True),
        preferred_element_type=jnp.float32,
    )
    positions = lax.axis_index("frames") * frame_count + jnp.arange(frame_count, dtype=jnp.int32)
    live = positions < length
    gated = jnp.where(
        live[:, None], glu_pre[:, 0, :] * jax.nn.sigmoid(glu_pre[:, 1, :]), 0.0
    ).astype(jnp.bfloat16)
    padded = padded_2(gated, (("frames", 0),), KERNEL // 2)
    depth = jnp.zeros((frame_count, channels), jnp.float32)
    for tap_index in range(KERNEL):
        depth = depth + padded[tap_index : tap_index + frame_count].astype(jnp.float32) * dw_kernel[
            tap_index
        ].astype(jnp.float32)
    hidden = (depth * jax.nn.sigmoid(depth)).astype(jnp.bfloat16)
    conv_part = jnp.dot(
        hidden, lax.all_gather(w_pw, "fsdp", axis=1, tiled=True), preferred_element_type=jnp.float32
    )
    conv_half = lax.psum_scatter(
        conv_part.astype(jnp.bfloat16), "heads", scatter_dimension=1, tiled=True
    ).astype(jnp.float32)
    result = (stream_own.astype(jnp.float32) + conv_half).astype(jnp.bfloat16)
    return result[None]


def solution(mesh):
    in_specs = (
        P(("groups", "fsdp"), "frames", "heads"),
        P(("groups", "fsdp")),
        P(("frames", "fsdp"), "heads"),
        P(("frames", "fsdp"), "heads"),
        P(("frames", "fsdp"), "heads"),
        P("heads", ("frames", "fsdp")),
        P("fsdp", None, "heads"),
        P(None, "heads"),
        P("heads", "fsdp"),
    )
    out_specs = P(("groups", "fsdp"), "frames", "heads")
    return jax.shard_map(shards, mesh=mesh, in_specs=in_specs, out_specs=out_specs, check_vma=False)
```

profile of v0, /device:TPU:0, one launch (start us, length us, event | category | flops | bytes accessed | tf_op | source)
XLA Modules:
  0.0 307.6 jit_solution(13441506892905612474)
XLA Ops:
  7.4 0.7 all-gather.9.cloned.1.call-update
  8.1 0.7 all-gather.11.cloned.1.call-update
  8.9 0.7 all-gather.7.cloned.1.call-update
  9.6 0.5 all-gather.13.cloned.1.call-update
  10.2 2.6 all_gather.27
  12.9 0.3 fusion.13
  13.9 40.3 %all-gather.9.cloned.1.call-done = bf16[1536,384]{1,0:T(8,128)(2,1)} async-done(((bf16[192,384]{1,0:T(8,128)(2,1)}), bf16[1536,384]{1,0:T(8,128)(2,1)}) %all-gather.9.cloned.1.call-update) | async-done | bytes 1179664 | tf_op jit(solution)/shard_map/all_gather | solution.py:47
  54.2 1.8 convolution_convert_fusion.3
  56.0 18.1 %all_gather.31 = bf16[768,384]{1,0:T(8,128)(2,1)S(1)} all-gather(bf16[192,384]{1,0:T(8,128)(2,1)S(1)} %convolution_convert_fusion.3), channel_id=1, replica_groups=mesh['groups'=2,'frames'=4,'fsdp'=2,'heads'=2] {'frames'}, dimensions={0}, use_global_device_ids=true | all-gather | bytes 737280 | tf_op jit(solution)/shard_map/all_gather | solution.py:62
  74.4 22.4 %all-gather.11.cloned.1.call-done = bf16[1536,384]{1,0:T(8,128)(2,1)} async-done(((bf16[192,384]{1,0:T(8,128)(2,1)}), bf16[1536,384]{1,0:T(8,128)(2,1)}) %all-gather.11.cloned.1.call-update) | async-done | bytes 1179664 | tf_op jit(solution)/shard_map/all_gather | solution.py:46
  96.8 1.8 convolution_convert_fusion.2
  98.7 40.1 %all-gather.7.cloned.1.call-done = bf16[1536,384]{1,0:T(8,128)(2,1)} async-done(((bf16[192,384]{1,0:T(8,128)(2,1)}), bf16[1536,384]{1,0:T(8,128)(2,1)}) %all-gather.7.cloned.1.call-update) | async-done | bytes 1179664 | tf_op jit(solution)/shard_map/all_gather | solution.py:48
  138.8 1.8 convolution_convert_fusion.4
  140.6 18.1 %all_gather.29 = bf16[768,384]{1,0:T(8,128)(2,1)S(1)} all-gather(bf16[192,384]{1,0:T(8,128)(2,1)S(1)} %convolution_convert_fusion.4), channel_id=1, replica_groups=mesh['groups'=2,'frames'=4,'fsdp'=2,'heads'=2] {'frames'}, dimensions={0}, use_global_device_ids=true | all-gather | bytes 737280 | tf_op jit(solution)/shard_map/all_gather | solution.py:63
  158.9 0.6 bitcast_reduce_fusion
  159.5 0.7 fusion.2
  160.2 0.8 fusion.22
  161.0 20.3 %all-gather.13.cloned.1.call-done = bf16[384,1536]{0,1:T(8,128)(2,1)} async-done(((bf16[384,192]{0,1:T(8,128)(2,1)}), bf16[384,1536]{0,1:T(8,128)(2,1)}) %all-gather.13.cloned.1.call-update) | async-done | bytes 1179664 | tf_op jit(solution)/shard_map/all_gather | solution.py:83
  181.4 2.8 convolution_convert_fusion.1
  184.3 1.8 copy.17
  186.1 0.5 all-gather.17.cloned.1.call-update
  187.1 14.7 %all-reduce.2.cloned.1.call-done = bf16[192,1536]{1,0:T(8,128)(2,1)} async-done(((bf16[192,1536]{1,0:T(8,128)(2,1)}), bf16[192,1536]{1,0:T(8,128)(2,1)}) %all-reduce.2.cloned.1.call-update) | async-done | bytes 589840 | tf_op jit(solution)/shard_map/psum | solution.py:86
  201.8 1.3 convert_reduce_fusion
  203.1 0.3 fusion.11
  203.4 44.1 %all-gather.15.cloned.1.call-done = bf16[1536,2,768]{2,0,1:T(8,128)(2,1)} async-done(((bf16[768,2,768]{2,0,1:T(8,128)(2,1)}), bf16[1536,2,768]{2,0,1:T(8,128)(2,1)}) %all-gather.15.cloned.1.call-update) | async-done | bytes 4718608 | tf_op jit(solution)/shard_map/all_gather | solution.py:95
  247.5 3.5 %fusion.26 = f32[192,2,768]{2,0,1:T(8,128)S(1)} fusion(bf16[1536,2,768]{2,0,1:T(8,128)(2,1)} %all-gather.15.cloned.1.call-done, bf16[192,1536]{1,0:T(8,128)(2,1)S(1)} %get-tuple-element.37, f32[192]{0:T(256)S(1)} %add_rsqrt_fusion, f32[192]{0:T(256)S(1)} %broadcast_multiply_fusion), kind=kOutput, calls=%fused_computation.64 | convolution fusion | flops 907149312 | bytes 6489600 | tf_op jit(solution)/shard_map/td,dgc->tgc/dot_general | solution.py:92
  251.2 3.4 %collective-permute-start = (bf16[15,768]{1,0:T(8,128)(2,1)S(1)}, bf16[15,768]{1,0:T(8,128)(2,1)S(1)}, u32[]{:S(2)}, u32[]{:S(2)}) collective-permute-start(bf16[15,768]{1,0:T(8,128)(2,1)S(1)} %get-tuple-element.38), channel_id=1, source_target_pairs={{0,4},{4,8},{8,12},{1,5},{5,9},{9,13},{2,6},{6,10},{10,14},{3,7},{... | collective-permute-start | bytes 69128 | tf_op jit(solution)/shard_map/ppermute | solution.py:21
  254.6 1.3 collective-permute-start.1
  256.0 28.9 %all-gather.17.cloned.1.call-done = bf16[768,1536]{1,0:T(8,128)(2,1)} async-done(((bf16[768,768]{1,0:T(8,128)(2,1)}), bf16[768,1536]{1,0:T(8,128)(2,1)}) %all-gather.17.cloned.1.call-update) | async-done | bytes 2359312 | tf_op jit(solution)/shard_map/all_gather | solution.py:111
  284.8 5.5 %convolution_convert_fusion = bf16[192,1536]{1,0:T(8,128)(2,1)} fusion(bf16[768,1536]{1,0:T(8,128)(2,1)} %all-gather.17.cloned.1.call-done, bf16[192,768]{1,0:T(8,128)(2,1)S(1)} %fusion.36, bf16[15,768]{1,0:T(8,128)(2,1)S(1)} %collective-permute-done.1, bf16[15,768]{1,0:T(8,128)(2,1)S(1)} %collective-permute-done, f32[768]{0:T(1024)S(1)} %get-tuple-element.34, ...), kind=kOutput, calls=%fused_computation | convolution fusion | flops 480854016 | bytes 3385344 | tf_op jit(solution)/shard_map/dot_general | solution.py:110
  290.3 8.1 %reduce-scatter.2.cloned.1.call-done = bf16[192,768]{1,0:T(8,128)(2,1)} async-done(((bf16[192,1536]{1,0:T(8,128)(2,1)}), bf16[192,768]{1,0:T(8,128)(2,1)}) %reduce-scatter.2.cloned.1.call-update) | async-done | bytes 294928 | tf_op jit(solution)/shard_map/reduce_scatter | solution.py:113
  298.5 1.7 fusion.37
  (32 shorter events, 1.8 us)
Async XLA Ops:
  7.4 46.9 %all-gather.9.cloned.1.call-start = ((), (), s32[]{:S(2)}) async-start(), calls=%async_computation.2 | async-start | bytes 1327104 | tf_op jit(solution)/shard_map/all_gather | solution.py:47
  8.1 88.7 %all-gather.11.cloned.1.call-start = ((), (), s32[]{:S(2)}) async-start(), calls=%async_computation.3 | async-start | bytes 1327104 | tf_op jit(solution)/shard_map/all_gather | solution.py:46
  8.8 130.0 %all-gather.7.cloned.1.call-start = ((), (), s32[]{:S(2)}) async-start(), calls=%async_computation.1 | async-start | bytes 1327104 | tf_op jit(solution)/shard_map/all_gather | solution.py:48
  9.6 171.8 %all-gather.13.cloned.1.call-start = ((), (), s32[]{:S(2)}) async-start(), calls=%async_computation.4 | async-start | bytes 1327104 | tf_op jit(solution)/shard_map/all_gather | solution.py:83
  10.1 191.6 %all-reduce.2.cloned.1.call-start = ((), (), s32[]{:S(2)}) async-start(), calls=%async_computation.5 | async-start | bytes 1179648 | tf_op jit(solution)/shard_map/psum | solution.py:86
  181.4 2.9 copy-start
  184.2 63.2 %all-gather.15.cloned.1.call-start = ((), (), s32[]{:S(2)}) async-start(), calls=%async_computation.6 | async-start | bytes 7077888 | tf_op jit(solution)/shard_map/all_gather | solution.py:95
  186.1 0.8 copy-start.1
  186.1 98.7 %all-gather.17.cloned.1.call-start = ((), (), s32[]{:S(2)}) async-start(), calls=%async_computation.7 | async-start | bytes 3538944 | tf_op jit(solution)/shard_map/all_gather | solution.py:111
  186.7 111.8 %reduce-scatter.2.cloned.1.call-start = ((), (), s32[]{:S(2)}) async-start(), calls=%async_computation.8 | async-start | bytes 884736 | tf_op jit(solution)/shard_map/reduce_scatter | solution.py:113
  251.2 33.7 %collective-permute-start = (bf16[15,768]{1,0:T(8,128)(2,1)S(1)}, bf16[15,768]{1,0:T(8,128)(2,1)S(1)}, u32[]{:S(2)}, u32[]{:S(2)}) collective-permute-start(bf16[15,768]{1,0:T(8,128)(2,1)S(1)} %get-tuple-element.38), channel_id=1, source_target_pairs={{0,4},{4,8},{8,12},{1,5},{5,9},{9,13},{2,6},{6,10},{10,14},{3,7},{... | collective-permute-start | bytes 69128 | tf_op jit(solution)/shard_map/ppermute | solution.py:21
  254.6 30.3 %collective-permute-start.1 = (bf16[15,768]{1,0:T(8,128)(2,1)S(1)}, bf16[15,768]{1,0:T(8,128)(2,1)S(1)}, u32[]{:S(2)}, u32[]{:S(2)}) collective-permute-start(bf16[15,768]{1,0:T(8,128)(2,1)S(1)} %get-tuple-element.39), channel_id=1, source_target_pairs={{4,0},{8,4},{12,8},{5,1},{9,5},{13,9},{6,2},{10,6},{14,10},{7,3},{... | collective-permute-start | bytes 69128 | tf_op jit(solution)/shard_map/ppermute | solution.py:23
Sparse Core Ops, SparseCore 0:
  10.3 43.8 all-gather.8
  56.4 40.3 all-gather.10
  99.0 39.8 all-gather.6
  140.9 40.4 all-gather.12
  184.4 17.3 all-reduce.1
  290.5 7.9 reduce-scatter.1
Sparse Core Ops, SparseCore 1:
  186.3 61.2 all-gather.14
  248.9 35.9 all-gather.16
where the time goes:
time: 308 us
  waiting for transfers between devices  222 us (72%)
  blocking collectives  38.7 us (13%)
  matrix products  18.5 us (6%)
  between operations  15.7 us (5%)
  other arithmetic  5.05 us (2%)
  starting transfers between devices  4.97 us (2%)
    all_gather x1, waiting for transfers between devices, shards(): lax.all_gather(w_glu, 'fsdp', axis=0, tiled=True)  44.1 us
    all_gather x1, waiting for transfers between devices, shards(): lax.all_gather(w_key, ('frames', 'fsdp'), axis=0, tiled=True)  40.3 us
    all_gather x1, waiting for transfers between devices, shards(): lax.all_gather(w_value, ('frames', 'fsdp'), axis=0, tiled=True)  40.1 us
    all_gather x1, waiting for transfers between devices, shards(): lax.all_gather(w_pw, 'fsdp', axis=1, tiled=True)  28.9 us
    all_gather x1, waiting for transfers between devices, shards(): lax.all_gather(w_query, ('frames', 'fsdp'), axis=0, tiled=True)  22.4 us
    all_gather x1, waiting for transfers between devices, shards(): lax.all_gather(w_out, ('frames', 'fsdp'), axis=1, tiled=True)  20.3 us
    all_gather x1, blocking collectives, shards(): lax.all_gather(key_rows, 'frames', axis=0, tiled=True)  18.1 us
    all_gather x1, blocking collectives, shards(): lax.all_gather(value_rows, 'frames', axis=0, tiled=True)  18.1 us
  transfers between devices with their start and end apart: 10, of which 8 were waited for; matrix products, arithmetic and copies ran while one was open for 5% of the time, Pallas kernels for 0%

commit v1 on v0

--- a/solution.py
+++ b/solution.py
@@ -1,3 +1,4 @@
+import functools
 import math
 import jax
 import jax.numpy as jnp
@@ -8,6 +9,25 @@
 KERNEL = 31
 EPS = 1e-05
 NEG_FILL = -1e30
+
+
+def obtain_turns_by_axis(arr_in, bus_axis, pos_dim):
+    n_dev_all = jax.lax.axis_size(bus_axis)
+    src_i = 1
+    by_rank = [arr_in]
+    while src_i < n_dev_all:
+        mixed_arr = jax.lax.ppermute(
+            by_rank[src_i - 1],
+            axis_name=bus_axis,
+            perm=[(k0, (k0 - 1) % n_dev_all) for k0 in range(n_dev_all)],
+        )
+        by_rank.append(mixed_arr)
+        src_i = src_i + 1
+    outer = jnp.concatenate(by_rank, axis=pos_dim)
+    return jnp.roll(outer, jax.lax.axis_index(bus_axis) * arr_in.shape[pos_dim], axis=pos_dim)
+
+
+view_circles = functools.partial(obtain_turns_by_axis, bus_axis=("frames", "fsdp"), pos_dim=1)
 
 
 def padded_2(cells, sides, width):
@@ -78,11 +98,7 @@
         "qhk,khd->qhd", expo.astype(jnp.bfloat16), value_block, preferred_element_type=jnp.float32
     )
     context = (block_acc / new_sum[:, :, None]).reshape(frame_count, att_cols).astype(jnp.bfloat16)
-    partial_value = jnp.dot(
-        context,
-        lax.all_gather(w_out, ("frames", "fsdp"), axis=1, tiled=True),
-        preferred_element_type=jnp.float32,
-    )
+    partial_value = jnp.dot(context, view_circles(w_out), preferred_element_type=jnp.float32)
     total = lax.psum(partial_value.astype(jnp.bfloat16), "heads").astype(jnp.float32)
     stream_full = (full_rows.astype(jnp.float32) + total).astype(jnp.bfloat16)
     stream_own = lax.dynamic_slice_in_dim(stream_full, own_start, half_width, 1)

time: 308 us -> 294 us (0.955)
  waiting for transfers between devices: 222 us -> 159 us
  starting transfers between devices: 4.97 us -> 42.1 us
  local copies, waits for them, and re-layouts: 2.57 us -> 15.2 us
    all_gather x1, waiting for transfers between devices: 40.3 us -> 0.01 us  [shards(): lax.all_gather(w_key, ('frames', 'fsdp'), axis=0, tiled=True)]
    ppermute x0 -> x7, starting transfers between devices: none -> 37 us  [obtain_turns_by_axis(): jax.lax.ppermute(by_rank[src_i - 1], axis_name=bus_axis, perm=[(k0, (k0 -...]
    all_gather x1 -> x0, waiting for transfers between devices: 20.3 us -> none  [shards(): lax.all_gather(w_out, ('frames', 'fsdp'), axis=1, tiled=True)]
    ppermute x0 -> x7, waiting for transfers between devices: none -> 18.9 us  [obtain_turns_by_axis(): jax.lax.ppermute(by_rank[src_i - 1], axis_name=bus_axis, perm=[(k0, (k0 -...]
    all_gather x1, waiting for transfers between devices: 22.4 us -> 3.85 us  [shards(): lax.all_gather(w_query, ('frames', 'fsdp'), axis=0, tiled=True)]
    unnamed x5 -> x24, local copies, waits for them, and re-layouts: 1.9 us -> 12.3 us
  transfers between devices with their start and end apart: 10 -> 16, of which waited for: 8 -> 13; matrix products, arithmetic and copies ran while one was open for 5% -> 8% of each run, Pallas kernels for 0% -> 0%
where the time goes in v1:
time: 294 us; the launch traced here: 293 us
  waiting for transfers between devices  159 us (54%)
  starting transfers between devices  42.1 us (14%)
  blocking collectives  36.5 us (12%)
  matrix products  19.4 us (7%)
  between operations  15.4 us (5%)
  local copies, waits for them, and re-layouts  15.2 us (5%)
  other arithmetic  5.02 us (2%)
    all_gather x1, waiting for transfers between devices, shards(): lax.all_gather(w_glu, 'fsdp', axis=0, tiled=True)  44.1 us
    all_gather x1, waiting for transfers between devices, shards(): lax.all_gather(w_value, ('frames', 'fsdp'), axis=0, tiled=True)  38.9 us
    ppermute x7, starting transfers between devices, obtain_turns_by_axis(): jax.lax.ppermute(by_rank[src_i - 1], axis_name=bus_axis, perm=[(k0, (k0 -...  37 us
    all_gather x1, waiting for transfers between devices, shards(): lax.all_gather(w_pw, 'fsdp', axis=1, tiled=True)  28.7 us
    ppermute x7, waiting for transfers between devices, obtain_turns_by_axis(): jax.lax.ppermute(by_rank[src_i - 1], axis_name=bus_axis, perm=[(k0, (k0 -...  18.9 us
    all_gather x1, blocking collectives, shards(): lax.all_gather(key_rows, 'frames', axis=0, tiled=True)  17.8 us
    all_gather x1, blocking collectives, shards(): lax.all_gather(value_rows, 'frames', axis=0, tiled=True)  16.3 us
    psum x1, waiting for transfers between devices, shards(): lax.psum(partial_value.astype(jnp.bfloat16), 'heads').astype(jnp.float32)  15 us
  transfers between devices with their start and end apart: 16, of which 13 were waited for; matrix products, arithmetic and copies ran while one was open for 8% of the time, Pallas kernels for 0%

profile of v1, /device:TPU:0, one launch (start us, length us, event | category | flops | bytes accessed | tf_op | source)
XLA Modules:
  0.0 293.1 jit_solution(13743615551415547358)
XLA Ops:
  8.9 6.1 %collective-permute-start = (bf16[384,192]{0,1:T(8,128)(2,1)}, bf16[384,192]{0,1:T(8,128)(2,1)S(1)}, u32[]{:S(2)}, u32[]{:S(2)}) collective-permute-start(bf16[384,192]{0,1:T(8,128)(2,1)} %param.14), channel_id=1, source_target_pairs={{0,14},{2,0},{4,2},{6,4},{8,6},{10,8},{12,10},{14,12},{1,15},{3,1}... | collective-permute-start | bytes 442376 | tf_op jit(solution)/shard_map/ppermute | solution.py:19
  15.0 2.4 all_gather.24
  18.4 5.1 %collective-permute-start.1 = (bf16[384,192]{0,1:T(8,128)(2,1)S(1)}, bf16[384,192]{0,1:T(8,128)(2,1)S(1)}, u32[]{:S(2)}, u32[]{:S(2)}) collective-permute-start(bf16[384,192]{0,1:T(8,128)(2,1)S(1)} %collective-permute-done), channel_id=1, source_target_pairs={{0,14},{2,0},{4,2},{6,4},{8,6},{10,8},{12,10},{14,12},{1,15},{3,1}... | collective-permute-start | bytes 442376 | tf_op jit(solution)/shard_map/ppermute | solution.py:19
  23.7 4.1 %collective-permute-done.1 = bf16[384,192]{0,1:T(8,128)(2,1)S(1)} collective-permute-done((bf16[384,192]{0,1:T(8,128)(2,1)S(1)}, bf16[384,192]{0,1:T(8,128)(2,1)S(1)}, u32[]{:S(2)}, u32[]{:S(2)}) %collective-permute-start.1) | collective-permute-done | bytes 147488 | tf_op jit(solution)/shard_map/ppermute | solution.py:19
  27.9 5.2 %collective-permute-start.2 = (bf16[384,192]{0,1:T(8,128)(2,1)S(1)}, bf16[384,192]{0,1:T(8,128)(2,1)S(1)}, u32[]{:S(2)}, u32[]{:S(2)}) collective-permute-start(bf16[384,192]{0,1:T(8,128)(2,1)S(1)} %collective-permute-done.1), channel_id=1, source_target_pairs={{0,14},{2,0},{4,2},{6,4},{8,6},{10,8},{12,10},{14,12},{1,15},{3,1}... | collective-permute-start | bytes 442376 | tf_op jit(solution)/shard_map/ppermute | solution.py:19
  33.1 2.7 collective-permute-done.2
  35.7 5.2 %collective-permute-start.3 = (bf16[384,192]{0,1:T(8,128)(2,1)S(1)}, bf16[384,192]{0,1:T(8,128)(2,1)S(1)}, u32[]{:S(2)}, u32[]{:S(2)}) collective-permute-start(bf16[384,192]{0,1:T(8,128)(2,1)S(1)} %collective-permute-done.2), channel_id=1, source_target_pairs={{0,14},{2,0},{4,2},{6,4},{8,6},{10,8},{12,10},{14,12},{1,15},{3,1}... | collective-permute-start | bytes 442376 | tf_op jit(solution)/shard_map/ppermute | solution.py:19
  41.6 4.9 %collective-permute-done.3 = bf16[384,192]{0,1:T(8,128)(2,1)S(1)} collective-permute-done((bf16[384,192]{0,1:T(8,128)(2,1)S(1)}, bf16[384,192]{0,1:T(8,128)(2,1)S(1)}, u32[]{:S(2)}, u32[]{:S(2)}) %collective-permute-start.3) | collective-permute-done | bytes 147488 | tf_op jit(solution)/shard_map/ppermute | solution.py:19
  46.5 5.2 %collective-permute-start.4 = (bf16[384,192]{0,1:T(8,128)(2,1)S(1)}, bf16[384,192]{0,1:T(8,128)(2,1)S(1)}, u32[]{:S(2)}, u32[]{:S(2)}) collective-permute-start(bf16[384,192]{0,1:T(8,128)(2,1)S(1)} %collective-permute-done.3), channel_id=1, source_target_pairs={{0,14},{2,0},{4,2},{6,4},{8,6},{10,8},{12,10},{14,12},{1,15},{3,1}... | collective-permute-start | bytes 442376 | tf_op jit(solution)/shard_map/ppermute | solution.py:19
  53.1 3.5 %collective-permute-done.4 = bf16[384,192]{0,1:T(8,128)(2,1)S(1)} collective-permute-done((bf16[384,192]{0,1:T(8,128)(2,1)S(1)}, bf16[384,192]{0,1:T(8,128)(2,1)S(1)}, u32[]{:S(2)}, u32[]{:S(2)}) %collective-permute-start.4) | collective-permute-done | bytes 147488 | tf_op jit(solution)/shard_map/ppermute | solution.py:19
  56.5 5.2 %collective-permute-start.5 = (bf16[384,192]{0,1:T(8,128)(2,1)S(1)}, bf16[384,192]{0,1:T(8,128)(2,1)S(1)}, u32[]{:S(2)}, u32[]{:S(2)}) collective-permute-start(bf16[384,192]{0,1:T(8,128)(2,1)S(1)} %collective-permute-done.4), channel_id=1, source_target_pairs={{0,14},{2,0},{4,2},{6,4},{8,6},{10,8},{12,10},{14,12},{1,15},{3,1}... | collective-permute-start | bytes 442376 | tf_op jit(solution)/shard_map/ppermute | solution.py:19
  63.1 2.1 collective-permute-done.5
  65.2 5.2 %collective-permute-start.6 = (bf16[384,192]{0,1:T(8,128)(2,1)S(1)}, bf16[384,192]{0,1:T(8,128)(2,1)S(1)}, u32[]{:S(2)}, u32[]{:S(2)}) collective-permute-start(bf16[384,192]{0,1:T(8,128)(2,1)S(1)} %collective-permute-done.5), channel_id=1, source_target_pairs={{0,14},{2,0},{4,2},{6,4},{8,6},{10,8},{12,10},{14,12},{1,15},{3,1}... | collective-permute-start | bytes 442376 | tf_op jit(solution)/shard_map/ppermute | solution.py:19
  79.2 1.8 convolution_convert_fusion.3
  81.0 17.8 %all_gather.28 = bf16[768,384]{1,0:T(8,128)(2,1)S(1)} all-gather(bf16[192,384]{1,0:T(8,128)(2,1)S(1)} %convolution_convert_fusion.3), channel_id=1, replica_groups=mesh['groups'=2,'frames'=4,'fsdp'=2,'heads'=2] {'frames'}, dimensions={0}, use_global_device_ids=true | all-gather | bytes 737280 | tf_op jit(solution)/shard_map/all_gather | solution.py:82
  99.0 3.8 %all-gather.10.cloned.1.call-done = bf16[1536,384]{1,0:T(8,128)(2,1)} async-done(((bf16[192,384]{1,0:T(8,128)(2,1)}), bf16[1536,384]{1,0:T(8,128)(2,1)}) %all-gather.10.cloned.1.call-update) | async-done | bytes 1179664 | tf_op jit(solution)/shard_map/all_gather | solution.py:66
  102.9 1.8 convolution_convert_fusion.2
  105.5 1.5 bitcast_reduce_fusion
  107.0 38.9 %all-gather.6.cloned.1.call-done = bf16[1536,384]{1,0:T(8,128)(2,1)} async-done(((bf16[192,384]{1,0:T(8,128)(2,1)}), bf16[1536,384]{1,0:T(8,128)(2,1)}) %all-gather.6.cloned.1.call-update) | async-done | bytes 1179664 | tf_op jit(solution)/shard_map/all_gather | solution.py:68
  145.9 1.8 convolution_convert_fusion.4
  147.7 16.3 %all_gather.26 = bf16[768,384]{1,0:T(8,128)(2,1)S(1)} all-gather(bf16[192,384]{1,0:T(8,128)(2,1)S(1)} %convolution_convert_fusion.4), channel_id=1, replica_groups=mesh['groups'=2,'frames'=4,'fsdp'=2,'heads'=2] {'frames'}, dimensions={0}, use_global_device_ids=true | all-gather | bytes 737280 | tf_op jit(solution)/shard_map/all_gather | solution.py:83
  166.9 2.8 convolution_convert_fusion.1
  169.9 1.8 copy.17
  172.6 15.0 %all-reduce.2.cloned.1.call-done = bf16[192,1536]{1,0:T(8,128)(2,1)} async-done(((bf16[192,1536]{1,0:T(8,128)(2,1)}), bf16[192,1536]{1,0:T(8,128)(2,1)}) %all-reduce.2.cloned.1.call-update) | async-done | bytes 589840 | tf_op jit(solution)/shard_map/psum | solution.py:102
  189.2 44.1 %all-gather.12.cloned.1.call-done = bf16[1536,2,768]{2,0,1:T(8,128)(2,1)} async-done(((bf16[768,2,768]{2,0,1:T(8,128)(2,1)}), bf16[1536,2,768]{2,0,1:T(8,128)(2,1)}) %all-gather.12.cloned.1.call-update) | async-done | bytes 4718608 | tf_op jit(solution)/shard_map/all_gather | solution.py:111
  233.3 3.5 %fusion.27 = f32[192,2,768]{2,0,1:T(8,128)S(1)} fusion(bf16[1536,2,768]{2,0,1:T(8,128)(2,1)} %all-gather.12.cloned.1.call-done, bf16[192,1536]{1,0:T(8,128)(2,1)S(1)} %get-tuple-element.37, f32[192]{0:T(256)S(1)} %add_rsqrt_fusion, f32[192]{0:T(256)S(1)} %broadcast_multiply_fusion), kind=kOutput, calls=%fused_computation.65 | convolution fusion | flops 907149312 | bytes 6489600 | tf_op jit(solution)/shard_map/td,dgc->tgc/dot_general | solution.py:108
  237.0 3.4 %collective-permute-start.7 = (bf16[15,768]{1,0:T(8,128)(2,1)S(1)}, bf16[15,768]{1,0:T(8,128)(2,1)S(1)}, u32[]{:S(2)}, u32[]{:S(2)}) collective-permute-start(bf16[15,768]{1,0:T(8,128)(2,1)S(1)} %get-tuple-element.38), channel_id=1, source_target_pairs={{0,4},{4,8},{8,12},{1,5},{5,9},{9,13},{2,6},{6,10},{10,14},{3,7},{... | collective-permute-start | bytes 69128 | tf_op jit(solution)/shard_map/ppermute | solution.py:41
  240.4 1.5 collective-permute-start.8
  242.0 28.7 %all-gather.14.cloned.1.call-done = bf16[768,1536]{1,0:T(8,128)(2,1)} async-done(((bf16[768,768]{1,0:T(8,128)(2,1)}), bf16[768,1536]{1,0:T(8,128)(2,1)}) %all-gather.14.cloned.1.call-update) | async-done | bytes 2359312 | tf_op jit(solution)/shard_map/all_gather | solution.py:127
  270.7 5.5 %convolution_convert_fusion = bf16[192,1536]{1,0:T(8,128)(2,1)} fusion(bf16[768,1536]{1,0:T(8,128)(2,1)} %all-gather.14.cloned.1.call-done, bf16[192,768]{1,0:T(8,128)(2,1)S(1)} %fusion.37, bf16[15,768]{1,0:T(8,128)(2,1)S(1)} %collective-permute-done.8, bf16[15,768]{1,0:T(8,128)(2,1)S(1)} %collective-permute-done.7, f32[768]{0:T(1024)S(1)} %get-tuple-element.34, ...), kind=kOutput, calls=%fused_computation | convolution fusion | flops 480854016 | bytes 3385344 | tf_op jit(solution)/shard_map/dot_general | solution.py:126
  276.1 8.1 %reduce-scatter.2.cloned.1.call-done = bf16[192,768]{1,0:T(8,128)(2,1)} async-done(((bf16[192,1536]{1,0:T(8,128)(2,1)}), bf16[192,768]{1,0:T(8,128)(2,1)}) %reduce-scatter.2.cloned.1.call-update) | async-done | bytes 294928 | tf_op jit(solution)/shard_map/reduce_scatter | solution.py:129
  284.3 1.7 fusion.38
  (63 shorter events, 21.2 us)
Async XLA Ops:
  7.4 33.5 %copy-start.2 = (bf16[384,192]{0,1:T(8,128)(2,1)S(1)}, bf16[384,192]{0,1:T(8,128)(2,1)}, u32[]{:S(2)}) copy-start(bf16[384,192]{0,1:T(8,128)(2,1)} %param.14) | copy-start | bytes 442372
  7.4 71.8 %all-gather.8.cloned.1.call-start = ((), (), s32[]{:S(2)}) async-start(), calls=%async_computation.2 | async-start | bytes 1327104 | tf_op jit(solution)/shard_map/all_gather | solution.py:67
  8.1 94.8 %all-gather.10.cloned.1.call-start = ((), (), s32[]{:S(2)}) async-start(), calls=%async_computation.3 | async-start | bytes 1327104 | tf_op jit(solution)/shard_map/all_gather | solution.py:66
  8.8 137.0 %all-gather.6.cloned.1.call-start = ((), (), s32[]{:S(2)}) async-start(), calls=%async_computation.1 | async-start | bytes 1327104 | tf_op jit(solution)/shard_map/all_gather | solution.py:68
  8.9 9.5 %collective-permute-start = (bf16[384,192]{0,1:T(8,128)(2,1)}, bf16[384,192]{0,1:T(8,128)(2,1)S(1)}, u32[]{:S(2)}, u32[]{:S(2)}) collective-permute-start(bf16[384,192]{0,1:T(8,128)(2,1)} %param.14), channel_id=1, source_target_pairs={{0,14},{2,0},{4,2},{6,4},{8,6},{10,8},{12,10},{14,12},{1,15},{3,1}... | collective-permute-start | bytes 442376 | tf_op jit(solution)/shard_map/ppermute | solution.py:19
  15.0 172.6 %all-reduce.2.cloned.1.call-start = ((), (), s32[]{:S(2)}) async-start(), calls=%async_computation.4 | async-start | bytes 1179648 | tf_op jit(solution)/shard_map/psum | solution.py:102
  18.4 9.5 %collective-permute-start.1 = (bf16[384,192]{0,1:T(8,128)(2,1)S(1)}, bf16[384,192]{0,1:T(8,128)(2,1)S(1)}, u32[]{:S(2)}, u32[]{:S(2)}) collective-permute-start(bf16[384,192]{0,1:T(8,128)(2,1)S(1)} %collective-permute-done), channel_id=1, source_target_pairs={{0,14},{2,0},{4,2},{6,4},{8,6},{10,8},{12,10},{14,12},{1,15},{3,1}... | collective-permute-start | bytes 442376 | tf_op jit(solution)/shard_map/ppermute | solution.py:19
  27.9 7.9 %collective-permute-start.2 = (bf16[384,192]{0,1:T(8,128)(2,1)S(1)}, bf16[384,192]{0,1:T(8,128)(2,1)S(1)}, u32[]{:S(2)}, u32[]{:S(2)}) collective-permute-start(bf16[384,192]{0,1:T(8,128)(2,1)S(1)} %collective-permute-done.1), channel_id=1, source_target_pairs={{0,14},{2,0},{4,2},{6,4},{8,6},{10,8},{12,10},{14,12},{1,15},{3,1}... | collective-permute-start | bytes 442376 | tf_op jit(solution)/shard_map/ppermute | solution.py:19
  35.7 10.8 %collective-permute-start.3 = (bf16[384,192]{0,1:T(8,128)(2,1)S(1)}, bf16[384,192]{0,1:T(8,128)(2,1)S(1)}, u32[]{:S(2)}, u32[]{:S(2)}) collective-permute-start(bf16[384,192]{0,1:T(8,128)(2,1)S(1)} %collective-permute-done.2), channel_id=1, source_target_pairs={{0,14},{2,0},{4,2},{6,4},{8,6},{10,8},{12,10},{14,12},{1,15},{3,1}... | collective-permute-start | bytes 442376 | tf_op jit(solution)/shard_map/ppermute | solution.py:19
  46.5 10.0 %collective-permute-start.4 = (bf16[384,192]{0,1:T(8,128)(2,1)S(1)}, bf16[384,192]{0,1:T(8,128)(2,1)S(1)}, u32[]{:S(2)}, u32[]{:S(2)}) collective-permute-start(bf16[384,192]{0,1:T(8,128)(2,1)S(1)} %collective-permute-done.3), channel_id=1, source_target_pairs={{0,14},{2,0},{4,2},{6,4},{8,6},{10,8},{12,10},{14,12},{1,15},{3,1}... | collective-permute-start | bytes 442376 | tf_op jit(solution)/shard_map/ppermute | solution.py:19
  56.5 8.7 %collective-permute-start.5 = (bf16[384,192]{0,1:T(8,128)(2,1)S(1)}, bf16[384,192]{0,1:T(8,128)(2,1)S(1)}, u32[]{:S(2)}, u32[]{:S(2)}) collective-permute-start(bf16[384,192]{0,1:T(8,128)(2,1)S(1)} %collective-permute-done.4), channel_id=1, source_target_pairs={{0,14},{2,0},{4,2},{6,4},{8,6},{10,8},{12,10},{14,12},{1,15},{3,1}... | collective-permute-start | bytes 442376 | tf_op jit(solution)/shard_map/ppermute | solution.py:19
  65.2 7.9 %collective-permute-start.6 = (bf16[384,192]{0,1:T(8,128)(2,1)S(1)}, bf16[384,192]{0,1:T(8,128)(2,1)S(1)}, u32[]{:S(2)}, u32[]{:S(2)}) collective-permute-start(bf16[384,192]{0,1:T(8,128)(2,1)S(1)} %collective-permute-done.5), channel_id=1, source_target_pairs={{0,14},{2,0},{4,2},{6,4},{8,6},{10,8},{12,10},{14,12},{1,15},{3,1}... | collective-permute-start | bytes 442376 | tf_op jit(solution)/shard_map/ppermute | solution.py:19
  165.1 1.1 copy-start.1
  166.9 2.9 %copy-start = (bf16[768,2,768]{2,1,0:T(2,128)(2,1)S(1)}, bf16[768,2,768]{2,1,0:T(2,128)(2,1)}, u32[]{:S(2)}) copy-start(bf16[768,2,768]{2,1,0:T(2,128)(2,1)} %param.15) | copy-start | bytes 7077892
  169.8 63.5 %all-gather.12.cloned.1.call-start = ((), (), s32[]{:S(2)}) async-start(), calls=%async_computation.5 | async-start | bytes 7077888 | tf_op jit(solution)/shard_map/all_gather | solution.py:111
  171.6 0.8 copy-start.3
  171.7 99.0 %all-gather.14.cloned.1.call-start = ((), (), s32[]{:S(2)}) async-start(), calls=%async_computation.6 | async-start | bytes 3538944 | tf_op jit(solution)/shard_map/all_gather | solution.py:127
  172.2 112.0 %reduce-scatter.2.cloned.1.call-start = ((), (), s32[]{:S(2)}) async-start(), calls=%async_computation.7 | async-start | bytes 884736 | tf_op jit(solution)/shard_map/reduce_scatter | solution.py:129
  237.0 33.7 %collective-permute-start.7 = (bf16[15,768]{1,0:T(8,128)(2,1)S(1)}, bf16[15,768]{1,0:T(8,128)(2,1)S(1)}, u32[]{:S(2)}, u32[]{:S(2)}) collective-permute-start(bf16[15,768]{1,0:T(8,128)(2,1)S(1)} %get-tuple-element.38), channel_id=1, source_target_pairs={{0,4},{4,8},{8,12},{1,5},{5,9},{9,13},{2,6},{6,10},{10,14},{3,7},{... | collective-permute-start | bytes 69128 | tf_op jit(solution)/shard_map/ppermute | solution.py:41
  240.4 30.3 %collective-permute-start.8 = (bf16[15,768]{1,0:T(8,128)(2,1)S(1)}, bf16[15,768]{1,0:T(8,128)(2,1)S(1)}, u32[]{:S(2)}, u32[]{:S(2)}) collective-permute-start(bf16[15,768]{1,0:T(8,128)(2,1)S(1)} %get-tuple-element.39), channel_id=1, source_target_pairs={{4,0},{8,4},{12,8},{5,1},{9,5},{13,9},{6,2},{10,6},{14,10},{7,3},{... | collective-permute-start | bytes 69128 | tf_op jit(solution)/shard_map/ppermute | solution.py:43
Sparse Core Ops, SparseCore 0:
  10.3 48.8 all-gather.7
  61.4 41.4 all-gather.9
  105.0 40.7 all-gather.5
  169.9 17.6 all-reduce.1
  276.3 7.9 reduce-scatter.1
Sparse Core Ops, SparseCore 1:
  171.8 61.4 all-gather.11
  234.7 35.9 all-gather.13
